TPU v7x, 32 devices: a whole 2x2x4 slice. The times are simulated.
32 devices in a mesh: dp: 8 (over y, x, core), tensor: 4 (over z).
Axes of the slice: x: 2, y: 2, z: 4, core: 2. Of those that a mesh axis runs over, the one named last changes fastest.
Arguments:
- hidden_in: bfloat16 [3, 4096, 768], P(None, ('dp', 'tensor')), may hold values from -6 to 6
- segment_ids: int32 [3, 32, 128], P(None, ('dp', 'tensor')), may hold values from 0 to 7, never falling along the last dimension, each value on 1 to 32 neighbouring positions
- pooled_grad: float32 [3, 32, 8, 768], P(None, ('dp', 'tensor')), may hold values from -96 to 96
- qkv_weight: bfloat16 [3, 768, 768], P(None, 'dp', 'tensor'), may hold values from -0.21875 to 0.21875
- qv_bias: bfloat16 [2, 768], P(None, ('dp', 'tensor')), may hold values from -1.1953125 to 1.1953125
- out_weight: bfloat16 [768, 768], P('tensor', 'dp'), may hold values from -0.875 to 0.875
- out_bias: bfloat16 [768], P(('dp', 'tensor')), may hold values from -1.1953125 to 1.1953125
- norm1_gain: bfloat16 [768], P(('dp', 'tensor')), may hold values from 0.099609375 to 1.8984375
- norm1_shift: bfloat16 [768], P(('dp', 'tensor')), may hold values from -1.1953125 to 1.1953125
- up_weight: bfloat16 [768, 3072], P('dp', 'tensor'), may hold values from -0.21875 to 0.21875
- up_bias: bfloat16 [3072], P(('dp', 'tensor')), may hold values from -1.1953125 to 1.1953125
- down_weight: bfloat16 [3072, 768], P('tensor', 'dp'), may hold values from -0.109375 to 0.109375
- down_bias: bfloat16 [768], P(('dp', 'tensor')), may hold values from -1.1953125 to 1.1953125
- norm2_gain: bfloat16 [768], P(('dp', 'tensor')), may hold values from 0.099609375 to 1.8984375
- norm2_shift: bfloat16 [768], P(('dp', 'tensor')), may hold values from -1.1953125 to 1.1953125
Outputs:
- pooled_out: float32 [3, 32, 8, 768], P(None, ('dp', 'tensor'))
- input_grad: float32 [3, 4096, 768], P(None, ('dp', 'tensor'))
- qkv_weight_grad: float32 [3, 768, 768], P(None, 'dp', 'tensor')
- qv_bias_grad: float32 [2, 768], P(None, ('dp', 'tensor'))
- out_weight_grad: float32 [768, 768], P('tensor', 'dp')
- out_bias_grad: float32 [768], P(('dp', 'tensor'))
- norm1_gain_grad: float32 [768], P(('dp', 'tensor'))
- norm1_shift_grad: float32 [768], P(('dp', 'tensor'))
- up_weight_grad: float32 [768, 3072], P('dp', 'tensor')
- up_bias_grad: float32 [3072], P(('dp', 'tensor'))
- down_weight_grad: float32 [3072, 768], P('tensor', 'dp')
- down_bias_grad: float32 [768], P(('dp', 'tensor'))
- norm2_gain_grad: float32 [768], P(('dp', 'tensor'))
- norm2_shift_grad: float32 [768], P(('dp', 'tensor'))
Inputs may be any that keep to these rules, and one draw needn't show every extreme that they name: `segment_ids`: in every row of 128 tokens the segment numbers never fall, each number from 0 to 7 occurs on 1 to 32 consecutive tokens, and some sentence has exactly 32 tokens.
All inputs are finite; a program needn't handle non-finite values.
Results may differ from a plain program's by a relative error of at most 0.013.
Values may be sent and summed in bfloat16 or wider, within the bound.
No kernel may reach another device: no remote copies, remote signals or barrier semaphores. Data moves between devices by JAX's collectives and lax.ppermute only.
A program may use at most 128 MiB of HBM per device.

v0:
```python
from functools import partial
import jax
import jax.numpy as jnp
from jax import lax
from jax.sharding import PartitionSpec as P

HD = 64
EPS = 1e-12
NEG = -1000000000.0
highest = lax.Precision.HIGHEST


def round_low(values):
    return lax.optimization_barrier(values.astype(jnp.bfloat16)).astype(jnp.float32)


def normalize(values, gain, shift):
    center = values - jnp.mean(values, axis=-1, keepdims=True)
    inverse = lax.rsqrt(jnp.mean(center * center, axis=-1, keepdims=True) + EPS)
    normed = center * inverse
    return (normed * gain + shift, normed, inverse)


def normalize_back(grad_out, normed, inverse, gain):
    scaled = grad_out * gain
    grad_in = inverse * (
        scaled
        - jnp.mean(scaled, axis=-1, keepdims=True)
        - normed * jnp.mean(scaled * normed, axis=-1, keepdims=True)
    )
    return (grad_in, jnp.sum(grad_out * normed, axis=0), jnp.sum(grad_out, axis=0))


def block_size(seq_count, seq_len):
    largest = max(1, 512 // seq_len)
    chosen = 1
    for trial in range(1, seq_count + 1):
        if seq_count % trial == 0 and trial <= largest:
            chosen = trial
    return chosen


def masked_scores(query_blk, key_blk, seg_blk, score_scale):
    raw_scores = (
        jnp.einsum("gqhd,gkhd->ghqk", query_blk, key_blk, preferred_element_type=jnp.float32)
        * score_scale
    )
    same_segment = seg_blk[:, None, :, None] == seg_blk[:, None, None, :]
    return jnp.where(same_segment, raw_scores, NEG)


def per_device(
    hidden_in,
    segment_ids,
    pooled_grad,
    qkv_weight,
    qv_bias,
    out_weight,
    out_bias,
    norm1_gain,
    norm1_shift,
    up_weight,
    up_bias,
    down_weight,
    down_bias,
    norm2_gain,
    norm2_shift,
):
    micro_total = hidden_in.shape[0]
    rows_local = hidden_in.shape[1]
    model_width = hidden_in.shape[2]
    seq_len = segment_ids.shape[2]
    seqs_local = segment_ids.shape[1]
    seg_count = pooled_grad.shape[2]
    tensor_rank = lax.axis_index("tensor")
    score_scale = float(HD) ** (-0.5)
    gathered = (
        lax.all_gather(qv_bias, ("dp", "tensor"), axis=1, tiled=True),
        lax.all_gather(out_bias, ("dp", "tensor"), axis=0, tiled=True),
        lax.all_gather(norm1_gain, ("dp", "tensor"), axis=0, tiled=True),
        lax.all_gather(norm1_shift, ("dp", "tensor"), axis=0, tiled=True),
        lax.all_gather(up_bias, ("dp", "tensor"), axis=0, tiled=True),
        lax.all_gather(down_bias, ("dp", "tensor"), axis=0, tiled=True),
        lax.all_gather(norm2_gain, ("dp", "tensor"), axis=0, tiled=True),
        lax.all_gather(norm2_shift, ("dp", "tensor"), axis=0, tiled=True),
    )
    qv_full, bias_out, gain_one, shift_one, up_full, bias_down, gain_two, shift_two = tuple(
        (item.astype(jnp.float32) for item in gathered)
    )
    head_cols = qkv_weight.shape[2]
    hidden_cols = up_weight.shape[1]
    heads_local = head_cols // HD
    bias_query = lax.dynamic_slice_in_dim(qv_full[0], tensor_rank * head_cols, head_cols)
    bias_value = lax.dynamic_slice_in_dim(qv_full[1], tensor_rank * head_cols, head_cols)
    bias_up = lax.dynamic_slice_in_dim(up_full, tensor_rank * hidden_cols, hidden_cols)

    def fetch_weights():
        return (
            lax.all_gather(qkv_weight, "dp", axis=1, tiled=True),
            lax.all_gather(out_weight, "dp", axis=1, tiled=True),
            lax.all_gather(up_weight, "dp", axis=0, tiled=True),
            lax.all_gather(down_weight, "dp", axis=1, tiled=True),
        )

    full_shapes = (
        (3, model_width, head_cols),
        (head_cols, model_width),
        (model_width, hidden_cols),
        (hidden_cols, model_width),
    )
    totals = tuple((jnp.zeros(shape_now, jnp.float32) for shape_now in full_shapes))
    qv_grad_local = jnp.zeros((2, head_cols), jnp.float32)
    up_bias_local = jnp.zeros((hidden_cols,), jnp.float32)
    out_bias_part = jnp.zeros((model_width,), jnp.float32)
    down_bias_part = jnp.zeros((model_width,), jnp.float32)
    gain_one_part = jnp.zeros((model_width,), jnp.float32)
    shift_one_part = jnp.zeros((model_width,), jnp.float32)
    gain_two_part = jnp.zeros((model_width,), jnp.float32)
    shift_two_part = jnp.zeros((model_width,), jnp.float32)
    pooled_list = []
    input_list = []
    for batch_index in range(micro_total):
        qkv_now, out_now, up_now, down_now = fetch_weights()
        x_rows = hidden_in[batch_index]
        seg_rows = segment_ids[batch_index]
        x_group, seg_group = (
            lax.all_gather(x_rows, "tensor", axis=0, tiled=True),
            lax.all_gather(seg_rows, "tensor", axis=0, tiled=True),
        )
        tokens_all = x_group.shape[0]
        projected = jnp.einsum("rd,cde->cre", x_group, qkv_now, preferred_element_type=jnp.float32)
        query_rows = (projected[0] + bias_query).astype(jnp.bfloat16)
        key_rows = projected[1].astype(jnp.bfloat16)
        value_rows = (projected[2] + bias_value).astype(jnp.bfloat16)
        seq_group = seg_group.shape[0]
        per_block = block_size(seq_group, seq_len)
        block_total = seq_group // per_block

        def split_heads(tensor_in):
            return tensor_in.reshape(block_total, per_block, seq_len, heads_local, HD)

        seg_blocks = seg_group.reshape(block_total, per_block, seq_len)
        query_blocks = split_heads(query_rows)
        key_blocks = split_heads(key_rows)
        value_blocks = split_heads(value_rows)

        def attend_forward(inputs):
            query_blk, key_blk, value_blk, seg_blk = inputs
            scores = masked_scores(query_blk, key_blk, seg_blk, score_scale)
            row_max = jnp.max(scores, axis=-1, keepdims=True)
            exp_scores = jnp.exp(scores - row_max)
            row_sum = jnp.sum(exp_scores, axis=-1, keepdims=True)
            prob_low = (exp_scores / row_sum).astype(jnp.bfloat16)
            attended_blk = jnp.einsum(
                "ghqk,gkhd->gqhd", prob_low, value_blk, preferred_element_type=jnp.float32
            )
            return (attended_blk.astype(jnp.bfloat16), (row_max + jnp.log(row_sum))[..., 0])

        attended, lse_blocks = lax.map(
            attend_forward, (query_blocks, key_blocks, value_blocks, seg_blocks)
        )
        att_rows = attended.reshape(tokens_all, head_cols)
        branch_one = lax.psum_scatter(
            jnp.dot(att_rows, out_now, preferred_element_type=jnp.float32),
            "tensor",
            scatter_dimension=0,
            tiled=True,
        )
        pre_one = branch_one + bias_out + x_rows.astype(jnp.float32)
        out_one, normed_one, inverse_one = normalize(pre_one, gain_one, shift_one)
        normed_group = lax.all_gather(out_one.astype(jnp.bfloat16), "tensor", axis=0, tiled=True)
        up_act = jnp.dot(normed_group, up_now, preferred_element_type=jnp.float32) + bias_up
        hidden_act = jax.nn.gelu(up_act, approximate=False).astype(jnp.bfloat16)
        branch_two = lax.psum_scatter(
            jnp.dot(hidden_act, down_now, preferred_element_type=jnp.float32),
            "tensor",
            scatter_dimension=0,
            tiled=True,
        )
        pre_two = branch_two + bias_down + out_one
        out_two, normed_two, inverse_two = normalize(pre_two, gain_two, shift_two)
        onehot = (
            seg_rows[:, :, None] == jnp.arange(seg_count, dtype=jnp.int32)[None, None, :]
        ).astype(jnp.float32)
        counts = jnp.sum(onehot, axis=1)
        sums = jnp.einsum(
            "lts,ltd->lsd",
            onehot,
            out_two.reshape(seqs_local, seq_len, model_width),
            precision=highest,
        )
        pooled_list.append(sums / counts[:, :, None])
        grad_out = jnp.einsum(
            "lts,lsd->ltd", onehot, pooled_grad[batch_index] / counts[:, :, None], precision=highest
        ).reshape(rows_local, model_width)
        grad_pre_two, gain_two_now, shift_two_now = normalize_back(
            grad_out, normed_two, inverse_two, gain_two
        )
        gain_two_part = gain_two_part + gain_two_now
        shift_two_part = shift_two_part + shift_two_now
        down_bias_part = down_bias_part + jnp.sum(grad_pre_two, axis=0)
        qkv_back, out_back, up_back, down_back = fetch_weights()
        ffn_grad_group = lax.all_gather(
            grad_pre_two.astype(jnp.bfloat16), "tensor", axis=0, tiled=True
        )
        batch_down = jnp.einsum(
            "rf,rd->fd", hidden_act, ffn_grad_group, preferred_element_type=jnp.float32
        )
        hidden_grad = jnp.einsum(
            "rd,fd->rf", ffn_grad_group, down_back, preferred_element_type=jnp.float32
        )
        gelu_value, gelu_pull = jax.vjp(partial(jax.nn.gelu, approximate=False), up_act)
        up_grad = gelu_pull(hidden_grad)[0].astype(jnp.bfloat16)
        up_bias_local = up_bias_local + jnp.sum(up_grad.astype(jnp.float32), axis=0)
        batch_up = jnp.einsum(
            "rd,rf->df", normed_group, up_grad, preferred_element_type=jnp.float32
        )
        normed_back = lax.psum_scatter(
            jnp.einsum("rf,df->rd", up_grad, up_back, preferred_element_type=jnp.float32),
            "tensor",
            scatter_dimension=0,
            tiled=True,
        )
        normed_grad = round_low(normed_back) + grad_pre_two
        grad_pre_one, gain_one_now, shift_one_now = normalize_back(
            normed_grad, normed_one, inverse_one, gain_one
        )
        gain_one_part = gain_one_part + gain_one_now
        shift_one_part = shift_one_part + shift_one_now
        out_bias_part = out_bias_part + jnp.sum(grad_pre_one, axis=0)
        attn_grad_group = lax.all_gather(
            grad_pre_one.astype(jnp.bfloat16), "tensor", axis=0, tiled=True
        )
        batch_out = jnp.einsum(
            "re,rd->ed", att_rows, attn_grad_group, preferred_element_type=jnp.float32
        )
        att_grad = jnp.einsum(
            "rd,ed->re", attn_grad_group, out_back, preferred_element_type=jnp.float32
        ).astype(jnp.bfloat16)
        att_grad_blocks = split_heads(att_grad)

        def attend_backward(inputs):
            query_blk, key_blk, value_blk, seg_blk, lse_blk, grad_blk = inputs
            scores = masked_scores(query_blk, key_blk, seg_blk, score_scale)
            prob_rows = jnp.exp(scores - lse_blk[..., None])
            value_grad = jnp.einsum(
                "ghqk,gqhd->gkhd",
                prob_rows.astype(jnp.bfloat16),
                grad_blk,
                preferred_element_type=jnp.float32,
            )
            prob_grad = jnp.einsum(
                "gqhd,gkhd->ghqk", grad_blk, value_blk, preferred_element_type=jnp.float32
            )
            score_grad = prob_rows * (
                prob_grad - jnp.sum(prob_rows * prob_grad, axis=-1, keepdims=True)
            )
            score_low = score_grad.astype(jnp.bfloat16)
            query_grad = (
                jnp.einsum(
                    "ghqk,gkhd->gqhd", score_low, key_blk, preferred_element_type=jnp.float32
                )
                * score_scale
            )
            key_grad = (
                jnp.einsum(
                    "ghqk,gqhd->gkhd", score_low, query_blk, preferred_element_type=jnp.float32
                )
                * score_scale
            )
            return (
                query_grad.astype(jnp.bfloat16),
                key_grad.astype(jnp.bfloat16),
                value_grad.astype(jnp.bfloat16),
            )

        query_grads, key_grads, value_grads = lax.map(
            attend_backward,
            (query_blocks, key_blocks, value_blocks, seg_blocks, lse_blocks, att_grad_blocks),
        )
        qkv_grad = jnp.stack(
            [
                query_grads.reshape(tokens_all, head_cols),
                key_grads.reshape(tokens_all, head_cols),
                value_grads.reshape(tokens_all, head_cols),
            ]
        )
        qv_grad_local = qv_grad_local + jnp.stack(
            [
                jnp.sum(qkv_grad[0].astype(jnp.float32), axis=0),
                jnp.sum(qkv_grad[2].astype(jnp.float32), axis=0),
            ]
        )
        batch_qkv = jnp.einsum("rd,cre->cde", x_group, qkv_grad, preferred_element_type=jnp.float32)
        input_back = lax.psum_scatter(
            jnp.einsum(
                "cre,cde->rd", qkv_grad, qkv_back, preferred_element_type=jnp.float32
            ).astype(jnp.bfloat16),
            "tensor",
            scatter_dimension=0,
            tiled=True,
        ).astype(jnp.float32)
        input_list.append(input_back + grad_pre_one)
        totals = tuple(
            (
                running + update
                for running, update in zip(totals, (batch_qkv, batch_out, batch_up, batch_down))
            )
        )
    final_qkv = lax.psum_scatter(totals[0], "dp", scatter_dimension=1, tiled=True)
    final_out = lax.psum_scatter(totals[1], "dp", scatter_dimension=1, tiled=True)
    final_up = lax.psum_scatter(totals[2], "dp", scatter_dimension=0, tiled=True)
    final_down = lax.psum_scatter(totals[3], "dp", scatter_dimension=1, tiled=True)
    qv_place = lax.dynamic_update_slice_in_dim(
        jnp.zeros((2, model_width), jnp.float32), qv_grad_local, tensor_rank * head_cols, 1
    )
    up_place = lax.dynamic_update_slice_in_dim(
        jnp.zeros(up_full.shape, jnp.float32), up_bias_local, tensor_rank * hidden_cols, 0
    )
    vector_out = (
        lax.psum_scatter(qv_place, ("dp", "tensor"), scatter_dimension=1, tiled=True),
        lax.psum_scatter(out_bias_part, ("dp", "tensor"), scatter_dimension=0, tiled=True),
        lax.psum_scatter(gain_one_part, ("dp", "tensor"), scatter_dimension=0, tiled=True),
        lax.psum_scatter(shift_one_part, ("dp", "tensor"), scatter_dimension=0, tiled=True),
        lax.psum_scatter(up_place, ("dp", "tensor"), scatter_dimension=0, tiled=True),
        lax.psum_scatter(down_bias_part, ("dp", "tensor"), scatter_dimension=0, tiled=True),
        lax.psum_scatter(gain_two_part, ("dp", "tensor"), scatter_dimension=0, tiled=True),
        lax.psum_scatter(shift_two_part, ("dp", "tensor"), scatter_dimension=0, tiled=True),
    )
    return (
        jnp.stack(pooled_list),
        jnp.stack(input_list),
        final_qkv,
        vector_out[0],
        final_out,
        vector_out[1],
        vector_out[2],
        vector_out[3],
        final_up,
        vector_out[4],
        final_down,
        vector_out[5],
        vector_out[6],
        vector_out[7],
    )


def solution(mesh):
    return jax.shard_map(
        per_device,
        mesh=mesh,
        in_specs=(
            P(None, ("dp", "tensor"), None),
            P(None, ("dp", "tensor"), None),
            P(None, ("dp", "tensor"), None, None),
            P(None, "dp", "tensor"),
            P(None, ("dp", "tensor")),
            P("tensor", "dp"),
            P(("dp", "tensor")),
            P(("dp", "tensor")),
            P(("dp", "tensor")),
            P("dp", "tensor"),
            P(("dp", "tensor")),
            P("tensor", "dp"),
            P(("dp", "tensor")),
            P(("dp", "tensor")),
            P(("dp", "tensor")),
        ),
        out_specs=(
            P(None, ("dp", "tensor"), None, None),
            P(None, ("dp", "tensor"), None),
            P(None, "dp", "tensor"),
            P(None, ("dp", "tensor")),
            P("tensor", "dp"),
            P(("dp", "tensor")),
            P(("dp", "tensor")),
            P(("dp", "tensor")),
            P("dp", "tensor"),
            P(("dp", "tensor")),
            P("tensor", "dp"),
            P(("dp", "tensor")),
            P(("dp", "tensor")),
            P(("dp", "tensor")),
        ),
        check_vma=False,
    )
```

profile of v0, /device:TPU:0, one launch (start us, length us, event | category | flops | bytes accessed | tf_op | source)
XLA Modules:
  0.0 912.5 jit_solution(8620162350987136270)
XLA Ops:
  10.9 21.3 %all-gather.4 = bf16[1,512,768]{2,1,0:T(8,128)(2,1)S(1)} all-gather(bf16[1,128,768]{2,1,0:T(8,128)(2,1)S(1)} %get-tuple-element.326), channel_id=6, replica_groups=mesh['dp'=8,'tensor'=4] {'tensor'}, dimensions={1}, use_global_device_ids=true | all-gather | bytes 983040 | tf_op jit(solution)/shard_map/all_gather | solution.py:127
  32.2 13.2 %all_gather.101 = bf16[3,768,192]{2,0,1:T(4,128)(2,1)S(1)} all-gather(bf16[3,96,192]{2,0,1:T(4,128)(2,1)S(1)} %copy.216), channel_id=1, replica_groups=mesh['dp'=8,'tensor'=4] {'dp'}, dimensions={1}, use_global_device_ids=true | all-gather | bytes 995328 | tf_op jit(solution)/shard_map/all_gather | solution.py:99
  47.5 9.2 %all-gather.5 = s32[4,1,128]{2,1,0:T(1,128)S(1)} all-gather(s32[1,1,128]{2,1,0:T(1,128)S(1)} %get-tuple-element.363), channel_id=7, replica_groups=mesh['dp'=8,'tensor'=4] {'tensor'}, dimensions={0}, use_global_device_ids=true | all-gather | bytes 2560 | tf_op jit(solution)/shard_map/all_gather | solution.py:128
  56.7 63.3 %all-gather.6 = bf16[32,24,2]{1,2,0:T(2,128)(2,1)S(1)} all-gather(bf16[1,24,2]{1,2,0:T(2,128)(2,1)S(1)} %bitcast.271), channel_id=1, replica_groups=mesh['dp'=8,'tensor'=4] {'dp','tensor'}, dimensions={0}, use_global_device_ids=true | all-gather | bytes 3168 | tf_op jit(solution)/shard_map/all_gather | solution.py:78
  121.5 8.4 all_gather.105
  135.7 27.2 %all-gather.2 = bf16[1,512,768]{2,1,0:T(8,128)(2,1)S(1)} all-gather(bf16[1,128,768]{2,1,0:T(8,128)(2,1)S(1)} %copy-done.79), channel_id=4, replica_groups=mesh['dp'=8,'tensor'=4] {'tensor'}, dimensions={1}, use_global_device_ids=true | all-gather | bytes 983040 | tf_op jit(solution)/shard_map/all_gather | solution.py:127
  166.5 12.2 %all-gather.3 = s32[4,1,128]{2,1,0:T(1,128)S(1)} all-gather(s32[1,1,128]{2,1,0:T(1,128)S(1)} %copy-done.149), channel_id=5, replica_groups=mesh['dp'=8,'tensor'=4] {'tensor'}, dimensions={0}, use_global_device_ids=true | all-gather | bytes 2560 | tf_op jit(solution)/shard_map/all_gather | solution.py:128
  182.2 22.7 %all-gather = bf16[1,512,768]{2,1,0:T(8,128)(2,1)S(1)} all-gather(bf16[1,128,768]{2,1,0:T(8,128)(2,1)S(1)} %get-tuple-element.325), channel_id=2, replica_groups=mesh['dp'=8,'tensor'=4] {'tensor'}, dimensions={1}, use_global_device_ids=true | all-gather | bytes 983040 | tf_op jit(solution)/shard_map/all_gather | solution.py:127
  211.0 11.9 %all-gather.1 = s32[4,1,128]{2,1,0:T(1,128)S(1)} all-gather(s32[1,1,128]{2,1,0:T(1,128)S(1)} %copy-done.148), channel_id=3, replica_groups=mesh['dp'=8,'tensor'=4] {'tensor'}, dimensions={0}, use_global_device_ids=true | all-gather | bytes 2560 | tf_op jit(solution)/shard_map/all_gather | solution.py:128
  229.8 40.1 %all-reduce.16 = (bf16[768]{0:T(1024)(128)(2,1)S(1)}, bf16[768]{0:T(1024)(128)(2,1)S(1)}, bf16[768]{0:T(1024)(128)(2,1)S(1)}, bf16[3072]{0:T(1024)(128)(2,1)S(1)...) all-reduce(bf16[768]{0:T(1024)(128)(2,1)S(1)} %dynamic-update-slice, ...), channel_id=1, replica_groups=mesh['dp'=8,'tensor'=4] {'dp','tensor'}, use_global_device_ids=true, to_apply=%add | all-reduce | flops 7680 | bytes 30720
  275.9 19.0 %all_gather.121 = bf16[512,768]{1,0:T(8,128)(2,1)} all-gather(bf16[128,768]{1,0:T(8,128)(2,1)S(1)} %get-tuple-element.334), channel_id=1, replica_groups=mesh['dp'=8,'tensor'=4] {'tensor'}, dimensions={0}, use_global_device_ids=true | all-gather | bytes 983040 | tf_op jit(solution)/shard_map/all_gather | solution.py:171
  294.9 7.2 multiply_convert_fusion
  305.7 23.8 %all_gather.118 = bf16[512,768]{1,0:T(8,128)(2,1)S(1)} all-gather(bf16[128,768]{1,0:T(8,128)(2,1)} %get-tuple-element.333), channel_id=1, replica_groups=mesh['dp'=8,'tensor'=4] {'tensor'}, dimensions={0}, use_global_device_ids=true | all-gather | bytes 983040 | tf_op jit(solution)/shard_map/all_gather | solution.py:171
  329.5 6.7 multiply_convert_fusion.1
  339.2 21.9 %all_gather.109 = bf16[512,768]{1,0:T(8,128)(2,1)S(1)} all-gather(bf16[128,768]{1,0:T(8,128)(2,1)} %get-tuple-element.332), channel_id=1, replica_groups=mesh['dp'=8,'tensor'=4] {'tensor'}, dimensions={0}, use_global_device_ids=true | all-gather | bytes 983040 | tf_op jit(solution)/shard_map/all_gather | solution.py:171
  361.1 6.9 multiply_convert_fusion.2
  378.5 12.4 %reduce-scatter.28.cloned.1.call-done = f32[128,768]{1,0:T(8,128)} async-done(((f32[512,768]{1,0:T(8,128)}), f32[128,768]{1,0:T(8,128)}) %reduce-scatter.28.cloned.1.call-update) | async-done | bytes 393232 | tf_op jit(solution)/shard_map/reduce_scatter | solution.py:174
  390.9 36.4 %reduce-scatter.24.cloned.1.call-done = f32[128,768]{1,0:T(8,128)} async-done(((f32[512,768]{1,0:T(8,128)}), f32[128,768]{1,0:T(8,128)}) %reduce-scatter.24.cloned.1.call-update) | async-done | bytes 393232 | tf_op jit(solution)/shard_map/reduce_scatter | solution.py:174
  435.1 18.1 %all_gather.126 = bf16[512,768]{1,0:T(8,128)(2,1)S(1)} all-gather(bf16[128,768]{1,0:T(8,128)(2,1)S(1)} %get-tuple-element.357), channel_id=1, replica_groups=mesh['dp'=8,'tensor'=4] {'tensor'}, dimensions={0}, use_global_device_ids=true | all-gather | bytes 983040 | tf_op jit(solution)/shard_map/all_gather | solution.py:203
  458.0 25.1 %all_gather.122 = bf16[512,768]{1,0:T(8,128)(2,1)S(1)} all-gather(bf16[128,768]{1,0:T(8,128)(2,1)} %get-tuple-element.291), channel_id=1, replica_groups=mesh['dp'=8,'tensor'=4] {'tensor'}, dimensions={0}, use_global_device_ids=true | all-gather | bytes 983040 | tf_op jit(solution)/shard_map/all_gather | solution.py:203
  490.4 23.0 %all_gather.124 = bf16[512,768]{1,0:T(8,128)(2,1)S(1)} all-gather(bf16[128,768]{1,0:T(8,128)(2,1)} %get-tuple-element.293), channel_id=1, replica_groups=mesh['dp'=8,'tensor'=4] {'tensor'}, dimensions={0}, use_global_device_ids=true | all-gather | bytes 983040 | tf_op jit(solution)/shard_map/all_gather | solution.py:203
  513.4 4.4 convert_reduce_fusion.1
  525.8 19.4 %reduce-scatter.34.cloned.1.call-done = f32[128,768]{1,0:T(8,128)} async-done(((f32[512,768]{1,0:T(8,128)}), f32[128,768]{1,0:T(8,128)}) %reduce-scatter.34.cloned.1.call-update) | async-done | bytes 393232 | tf_op jit(solution)/shard_map/reduce_scatter | solution.py:218
  549.9 31.9 %reduce-scatter.38.cloned.1.call-done = f32[128,768]{1,0:T(8,128)} async-done(((f32[512,768]{1,0:T(8,128)}), f32[128,768]{1,0:T(8,128)}) %reduce-scatter.38.cloned.1.call-update) | async-done | bytes 393232 | tf_op jit(solution)/shard_map/reduce_scatter | solution.py:218
  585.7 18.7 %all_gather.123 = bf16[512,768]{1,0:T(8,128)(2,1)S(1)} all-gather(bf16[128,768]{1,0:T(8,128)(2,1)S(1)} %convert_element_type.390), channel_id=1, replica_groups=mesh['dp'=8,'tensor'=4] {'tensor'}, dimensions={0}, use_global_device_ids=true | all-gather | bytes 983040 | tf_op jit(solution)/shard_map/all_gather | solution.py:231
  609.2 17.5 %all_gather.125 = bf16[512,768]{1,0:T(8,128)(2,1)S(1)} all-gather(bf16[128,768]{1,0:T(8,128)(2,1)S(1)} %convert_element_type.406), channel_id=1, replica_groups=mesh['dp'=8,'tensor'=4] {'tensor'}, dimensions={0}, use_global_device_ids=true | all-gather | bytes 983040 | tf_op jit(solution)/shard_map/all_gather | solution.py:231
  637.9 17.4 %all_gather.127 = bf16[512,768]{1,0:T(8,128)(2,1)S(1)} all-gather(bf16[128,768]{1,0:T(8,128)(2,1)} %convert_element_type.422), channel_id=1, replica_groups=mesh['dp'=8,'tensor'=4] {'tensor'}, dimensions={0}, use_global_device_ids=true | all-gather | bytes 983040 | tf_op jit(solution)/shard_map/all_gather | solution.py:231
  713.3 41.6 %all-reduce.15 = (f32[2,768]{1,0:T(2,128)S(1)}, f32[768]{0:T(1024)S(1)}, f32[768]{0:T(1024)S(1)}, f32[768]{0:T(1024)S(1)}, f32[3072]{0:T(1024)S(1)}, /*index=5*/...) all-reduce(f32[2,768]{1,0:T(2,128)S(1)} %dynamic_update_slice.38, ...), channel_id=21, replica_groups=mesh['dp'=8,'tensor'=4] {'dp','tensor'}, use_global_device_ids=true, to_apply=%region_55.56.clone | all-reduce | flops 9216 | bytes 73728
  763.3 6.1 reduce-scatter.44.cloned.1.call-done
  771.4 40.9 %reduce-scatter.50.cloned.1.call-done = f32[96,576]{1,0:T(8,128)} async-done(((f32[768,576]{1,0:T(8,128)}), f32[96,576]{1,0:T(8,128)}) %reduce-scatter.50.cloned.1.call-update) | async-done | bytes 221200
  814.2 44.6 %reduce-scatter.48.cloned.1.call-done = f32[768,96]{0,1:T(8,128)} async-done(((f32[768,768]{0,1:T(8,128)}), f32[768,96]{0,1:T(8,128)}) %reduce-scatter.48.cloned.1.call-update) | async-done | bytes 294928 | tf_op jit(solution)/shard_map/reduce_scatter | solution.py:313
  858.8 46.1 %reduce-scatter.46.cloned.1.call-done = f32[96,768]{1,0:T(8,128)} async-done(((f32[768,768]{1,0:T(8,128)}), f32[96,768]{1,0:T(8,128)}) %reduce-scatter.46.cloned.1.call-update) | async-done | bytes 294928 | tf_op jit(solution)/shard_map/reduce_scatter | solution.py:312
  (615 shorter events, 175.5 us)
Async XLA Ops:
  8.0 263.7 %reduce-scatter.30.cloned.1.call-start = ((), (), s32[]{:S(2)}) async-start(), calls=%async_computation.22 | async-start | bytes 1966080 | tf_op jit(solution)/shard_map/reduce_scatter | solution.py:163
  32.2 14.1 %copy-start.27 = (bf16[1,512,768]{2,1,0:T(8,128)(2,1)}, bf16[1,512,768]{2,1,0:T(8,128)(2,1)S(1)}, u32[]{:S(2)}) copy-start(bf16[1,512,768]{2,1,0:T(8,128)(2,1)S(1)} %all-gather.4) | copy-start | bytes 2359300
  45.4 117.5 %copy-start.58 = (bf16[3,768,192]{2,0,1:T(4,128)(2,1)}, bf16[3,768,192]{2,0,1:T(4,128)(2,1)S(1)}, u32[]{:S(2)}) copy-start(bf16[3,768,192]{2,0,1:T(4,128)(2,1)S(1)} %all_gather.101) | copy-start | bytes 2654212
  46.3 74.3 %copy-start.88 = (bf16[192,96]{1,0:T(8,128)(2,1)S(1)}, bf16[192,96]{1,0:T(8,128)(2,1)}, u32[]{:S(2)}) copy-start(bf16[192,96]{1,0:T(8,128)(2,1)} %param.20) | copy-start | bytes 110596
  135.6 136.2 %reduce-scatter.26.cloned.1.call-start = ((), (), s32[]{:S(2)}) async-start(), calls=%async_computation.20 | async-start | bytes 1966080 | tf_op jit(solution)/shard_map/reduce_scatter | solution.py:163
  166.3 14.0 %copy-start.65 = (f32[4,128,3,64]{1,0,3,2:T(4,128)}, f32[4,128,3,64]{1,0,3,2:T(4,128)S(1)}, u32[]{:S(2)}) copy-start(f32[4,128,3,64]{1,0,3,2:T(4,128)S(1)} %squeeze.124) | copy-start | bytes 1179652
  182.1 89.6 %reduce-scatter.22.cloned.1.call-start = ((), (), s32[]{:S(2)}) async-start(), calls=%async_computation.16 | async-start | bytes 1966080 | tf_op jit(solution)/shard_map/reduce_scatter | solution.py:163
  208.6 14.4 %copy-start.53 = (bf16[4,128,3,64]{1,0,3,2:T(4,128)(2,1)}, bf16[4,128,3,64]{1,0,3,2:T(4,128)(2,1)S(1)}, u32[]{:S(2)}) copy-start(bf16[4,128,3,64]{1,0,3,2:T(4,128)(2,1)S(1)} %convert_element_type.351) | copy-start | bytes 589828
  226.7 68.2 %all-gather.10.cloned.1.call-start = ((), (), s32[]{:S(2)}) async-start(), calls=%async_computation.17 | async-start | bytes 1327104 | tf_op jit(solution)/shard_map/all_gather | solution.py:101
  227.3 74.9 %all-gather.12.cloned.1.call-start = ((), (), s32[]{:S(2)}) async-start(), calls=%async_computation.18 | async-start | bytes 1327104 | tf_op jit(solution)/shard_map/all_gather | solution.py:102
  227.8 150.6 %reduce-scatter.32.cloned.1.call-start = ((), (), s32[]{:S(2)}) async-start(), calls=%async_computation.23 | async-start | bytes 1966080 | tf_op jit(solution)/shard_map/reduce_scatter | solution.py:174
  305.6 85.3 %reduce-scatter.28.cloned.1.call-start = ((), (), s32[]{:S(2)}) async-start(), calls=%async_computation.21 | async-start | bytes 1966080 | tf_op jit(solution)/shard_map/reduce_scatter | solution.py:174
  339.1 88.2 %reduce-scatter.24.cloned.1.call-start = ((), (), s32[]{:S(2)}) async-start(), calls=%async_computation.19 | async-start | bytes 1966080 | tf_op jit(solution)/shard_map/reduce_scatter | solution.py:174
  370.8 153.2 %reduce-scatter.42.cloned.1.call-start = ((), (), s32[]{:S(2)}) async-start(), calls=%async_computation.28 | async-start | bytes 1966080 | tf_op jit(solution)/shard_map/reduce_scatter | solution.py:218
  431.8 21.5 %copy-start.169 = (f32[512,768]{1,0:T(8,128)S(1)}, f32[512,768]{1,0:T(8,128)}, u32[]{:S(2)}) copy-start(f32[512,768]{1,0:T(8,128)} %get-tuple-element.373) | copy-start | bytes 4718596
  433.9 19.4 %copy-start.160 = (bf16[768,768]{0,1:T(8,128)(2,1)S(1)}, bf16[768,768]{0,1:T(8,128)(2,1)}, u32[]{:S(2)}) copy-start(bf16[768,768]{0,1:T(8,128)(2,1)} %all-gather.12.cloned.1.call-done) | copy-start | bytes 3538948
  433.9 19.4 %copy-start.168 = (f32[512,768]{1,0:T(8,128)S(1)}, f32[512,768]{1,0:T(8,128)}, u32[]{:S(2)}) copy-start(f32[512,768]{1,0:T(8,128)} %get-tuple-element.312) | copy-start | bytes 4718596
  457.9 87.3 %reduce-scatter.34.cloned.1.call-start = ((), (), s32[]{:S(2)}) async-start(), calls=%async_computation.24 | async-start | bytes 1966080 | tf_op jit(solution)/shard_map/reduce_scatter | solution.py:218
  490.4 91.4 %reduce-scatter.38.cloned.1.call-start = ((), (), s32[]{:S(2)}) async-start(), calls=%async_computation.26 | async-start | bytes 1966080 | tf_op jit(solution)/shard_map/reduce_scatter | solution.py:218
  520.7 239.0 %reduce-scatter.52.cloned.1.call-start = ((), (), s32[]{:S(2)}) async-start(), calls=%async_computation.33 | async-start | bytes 884736
  585.6 21.0 %copy-start.19 = (f32[128,768]{1,0:T(8,128)}, f32[128,768]{1,0:T(8,128)S(1)}, u32[]{:S(2)}) copy-start(f32[128,768]{1,0:T(8,128)S(1)} %get-tuple-element.288) | copy-start | bytes 1179652
  585.6 19.9 %copy-start.48 = (bf16[4,128,3,64]{1,0,3,2:T(4,128)(2,1)S(1)}, bf16[4,128,3,64]{1,0,3,2:T(4,128)(2,1)}, u32[]{:S(2)}) copy-start(bf16[4,128,3,64]{1,0,3,2:T(4,128)(2,1)} %copy-done.47) | copy-start | bytes 589828
  637.9 18.9 %copy-start.45 = (bf16[4,128,3,64]{1,0,3,2:T(4,128)(2,1)S(1)}, bf16[4,128,3,64]{1,0,3,2:T(4,128)(2,1)}, u32[]{:S(2)}) copy-start(bf16[4,128,3,64]{1,0,3,2:T(4,128)(2,1)} %copy-done.44) | copy-start | bytes 589828
  658.3 102.9 %reduce-scatter.40.cloned.1.call-start = ((), (), s32[]{:S(2)}) async-start(), calls=%async_computation.27 | async-start | bytes 983040 | tf_op jit(solution)/shard_map/reduce_scatter | solution.py:295
  673.2 89.1 %reduce-scatter.36.cloned.1.call-start = ((), (), s32[]{:S(2)}) async-start(), calls=%async_computation.25 | async-start | bytes 983040 | tf_op jit(solution)/shard_map/reduce_scatter | solution.py:295
  680.4 89.0 %reduce-scatter.44.cloned.1.call-start = ((), (), s32[]{:S(2)}) async-start(), calls=%async_computation.29 | async-start | bytes 983040 | tf_op jit(solution)/shard_map/reduce_scatter | solution.py:295
  684.5 127.8 %reduce-scatter.50.cloned.1.call-start = ((), (), s32[]{:S(2)}) async-start(), calls=%async_computation.32 | async-start | bytes 2211840
  695.6 163.3 %reduce-scatter.48.cloned.1.call-start = ((), (), s32[]{:S(2)}) async-start(), calls=%async_computation.31 | async-start | bytes 2654208 | tf_op jit(solution)/shard_map/reduce_scatter | solution.py:313
  701.5 203.5 %reduce-scatter.46.cloned.1.call-start = ((), (), s32[]{:S(2)}) async-start(), calls=%async_computation.30 | async-start | bytes 2654208 | tf_op jit(solution)/shard_map/reduce_scatter | solution.py:312
  707.7 53.6 %copy-start.24 = (f32[128,768]{1,0:T(8,128)S(1)}, f32[128,768]{1,0:T(8,128)}, u32[]{:S(2)}) copy-start(f32[128,768]{1,0:T(8,128)} %copy-done.23) | copy-start | bytes 1179652
  708.4 53.9 %copy-start.20 = (f32[128,768]{1,0:T(8,128)S(1)}, f32[128,768]{1,0:T(8,128)}, u32[]{:S(2)}) copy-start(f32[128,768]{1,0:T(8,128)} %copy-done.19) | copy-start | bytes 1179652
  710.5 58.8 %copy-start.22 = (f32[128,768]{1,0:T(8,128)S(1)}, f32[128,768]{1,0:T(8,128)}, u32[]{:S(2)}) copy-start(f32[128,768]{1,0:T(8,128)} %get-tuple-element.356) | copy-start | bytes 1179652
  (156 other events, 522.8 us)
Sparse Core Ops, SparseCore 0:
  135.7 43.5 reduce-scatter.29
  182.2 40.3 reduce-scatter.25
  226.8 34.0 reduce-scatter.21
  305.7 47.1 reduce-scatter.31
  355.1 35.7 reduce-scatter.27
  393.0 34.2 reduce-scatter.23
  458.1 49.3 reduce-scatter.41
  509.7 35.4 reduce-scatter.33
  547.5 34.2 reduce-scatter.37
Sparse Core Ops, SparseCore 1:
  229.0 21.3 all-gather.9
  252.1 23.9 all-gather.11
  658.4 35.3 reduce-scatter.51
  696.1 23.0 reduce-scatter.39
  721.5 23.4 reduce-scatter.35
  747.3 22.0 reduce-scatter.43
  772.6 39.7 reduce-scatter.49
  816.5 42.3 reduce-scatter.47
  862.6 42.3 reduce-scatter.45
where the time goes:
time: 922 us; the launch traced here: 913 us
  blocking collectives  456 us (49%)
  waiting for transfers between devices  239 us (26%)
  matrix products  103 us (11%)
  local copies, waits for them, and re-layouts  58.1 us (6%)
  other arithmetic  37.3 us (4%)
  between operations  18.2 us (2%)
    unnamed x2, blocking collectives  81.7 us
    all_gather x3, blocking collectives, per_device(): lax.all_gather(x_rows, 'tensor', axis=0, tiled=True)  71.3 us
    all_gather x3, blocking collectives, per_device(): lax.all_gather(grad_pre_two.astype(jnp.bfloat16), 'tensor', axis=0, tiled...  66.2 us
    all_gather x3, blocking collectives, per_device(): lax.all_gather(out_one.astype(jnp.bfloat16), 'tensor', axis=0, tiled=True)  64.7 us
    all_gather x1, blocking collectives, per_device(): lax.all_gather(qv_bias, ('dp', 'tensor'), axis=1, tiled=True)  63.3 us
    all_gather x3, blocking collectives, per_device(): lax.all_gather(grad_pre_one.astype(jnp.bfloat16), 'tensor', axis=0, tiled...  53.6 us
    reduce_scatter x3, waiting for transfers between devices, per_device(): lax.psum_scatter(jnp.einsum('rf,df->rd', up_grad, up_back, preferred_elem...  51.3 us
    reduce_scatter x3, waiting for transfers between devices, per_device(): lax.psum_scatter(jnp.dot(hidden_act, down_now, preferred_element_type=jnp...  48.9 us
  transfers between devices with their start and end apart: 18, of which 8 were waited for; matrix products, arithmetic and copies ran while one was open for 15% of the time, Pallas kernels for 0%

commit v1 on v0

--- a/solution.py
+++ b/solution.py
@@ -228,9 +228,24 @@
         gain_one_part = gain_one_part + gain_one_now
         shift_one_part = shift_one_part + shift_one_now
         out_bias_part = out_bias_part + jnp.sum(grad_pre_one, axis=0)
-        attn_grad_group = lax.all_gather(
-            grad_pre_one.astype(jnp.bfloat16), "tensor", axis=0, tiled=True
-        )
+        x = grad_pre_one.astype(jnp.bfloat16)
+        size, mine, rows = (lax.axis_size("tensor"), lax.axis_index("tensor"), x.shape[0])
+        right = [(i, (i + 1) % size) for i in range(size)]
+        behind = [(i, (i - 1) % size) for i in range(size)]
+        attn_grad_group = jnp.zeros((*x.shape[:0], size * rows, *x.shape[0 + 1 :]), x.dtype)
+        attn_grad_group = lax.dynamic_update_slice_in_dim(attn_grad_group, x, mine * rows, axis=0)
+        from_left = from_right = x
+        middle = size // 2
+        for step in range(1, middle + 1):
+            from_left = lax.ppermute(from_left, "tensor", right)
+            attn_grad_group = lax.dynamic_update_slice_in_dim(
+                attn_grad_group, from_left, (mine - step) % size * rows, axis=0
+            )
+            if step < size - middle:
+                from_right = lax.ppermute(from_right, "tensor", behind)
+                attn_grad_group = lax.dynamic_update_slice_in_dim(
+                    attn_grad_group, from_right, (mine + step) % size * rows, axis=0
+                )
         batch_out = jnp.einsum(
             "re,rd->ed", att_rows, attn_grad_group, preferred_element_type=jnp.float32
         )

time: 922 us -> 896 us (0.972)
  blocking collectives: 456 us -> 392 us
  starting transfers between devices: 1.11 us -> 18.6 us
  local copies, waits for them, and re-layouts: 58.1 us -> 75.3 us
    all_gather x3 -> x0, blocking collectives: 53.6 us -> none  [per_device(): lax.all_gather(grad_pre_one.astype(jnp.bfloat16), 'tensor', axis=0, tiled...]
    ppermute x0 -> x9, starting transfers between devices: none -> 17.1 us  [the longest x3 10.7 us: per_device(): from_right = lax.ppermute(from_right, 'tensor', behind)]
    ppermute x0 -> x9, waiting for transfers between devices: none -> 14.8 us  [the longest x6 14.8 us: per_device(): from_left = lax.ppermute(from_left, 'tensor', right)]
    unnamed x376 -> x386, local copies, waits for them, and re-layouts: 39 us -> 44.4 us
  transfers between devices with their start and end apart: 18 -> 27, of which waited for: 8 -> 12; matrix products, arithmetic and copies ran while one was open for 15% -> 18% of each run, Pallas kernels for 0% -> 0%
where the time goes in v1:
time: 896 us; the launch traced here: 886 us
  blocking collectives  392 us (44%)
  waiting for transfers between devices  242 us (27%)
  matrix products  98.5 us (11%)
  local copies, waits for them, and re-layouts  75.3 us (8%)
  other arithmetic  40.3 us (4%)
  starting transfers between devices  18.6 us (2%)
  between operations  18.5 us (2%)
    unnamed x2, blocking collectives  80.9 us
    all_gather x3, blocking collectives, per_device(): lax.all_gather(grad_pre_two.astype(jnp.bfloat16), 'tensor', axis=0, tiled...  66.7 us
    all_gather x1, blocking collectives, per_device(): lax.all_gather(qv_bias, ('dp', 'tensor'), axis=1, tiled=True)  65.5 us
    all_gather x3, blocking collectives, per_device(): lax.all_gather(out_one.astype(jnp.bfloat16), 'tensor', axis=0, tiled=True)  65 us
    all_gather x3, blocking collectives, per_device(): lax.all_gather(x_rows, 'tensor', axis=0, tiled=True)  64 us
    reduce_scatter x3, waiting for transfers between devices, per_device(): lax.psum_scatter(jnp.dot(hidden_act, down_now, preferred_element_type=jnp...  48.6 us
    reduce_scatter x1, waiting for transfers between devices, per_device(): lax.psum_scatter(totals[3], 'dp', scatter_dimension=1, tiled=True)  46.1 us
    reduce_scatter x3, waiting for transfers between devices, per_device(): lax.psum_scatter(jnp.einsum('rf,df->rd', up_grad, up_back, preferred_elem...  45.1 us
  transfers between devices with their start and end apart: 27, of which 12 were waited for; matrix products, arithmetic and copies ran while one was open for 18% of the time, Pallas kernels for 0%

profile of v1, /device:TPU:0, one launch (start us, length us, event | category | flops | bytes accessed | tf_op | source)
XLA Modules:
  0.0 885.9 jit_solution(8292244380391928972)
XLA Ops:
  10.0 21.3 %all-gather = bf16[1,512,768]{2,1,0:T(8,128)(2,1)S(1)} all-gather(bf16[1,128,768]{2,1,0:T(8,128)(2,1)S(1)} %get-tuple-element.331), channel_id=2, replica_groups=mesh['dp'=8,'tensor'=4] {'tensor'}, dimensions={1}, use_global_device_ids=true | all-gather | bytes 983040 | tf_op jit(solution)/shard_map/all_gather | solution.py:127
  31.4 13.2 %all_gather.92 = bf16[3,768,192]{2,0,1:T(4,128)(2,1)S(1)} all-gather(bf16[3,96,192]{2,0,1:T(4,128)(2,1)S(1)} %copy.216), channel_id=1, replica_groups=mesh['dp'=8,'tensor'=4] {'dp'}, dimensions={1}, use_global_device_ids=true | all-gather | bytes 995328 | tf_op jit(solution)/shard_map/all_gather | solution.py:99
  46.4 8.4 all_gather.96
  55.1 65.5 %all-gather.6 = bf16[32,24,2]{1,2,0:T(2,128)(2,1)S(1)} all-gather(bf16[1,24,2]{1,2,0:T(2,128)(2,1)S(1)} %bitcast.271), channel_id=1, replica_groups=mesh['dp'=8,'tensor'=4] {'dp','tensor'}, dimensions={0}, use_global_device_ids=true | all-gather | bytes 3168 | tf_op jit(solution)/shard_map/all_gather | solution.py:78
  122.3 7.5 all-gather.1
  134.4 23.2 %all-gather.2 = bf16[1,512,768]{2,1,0:T(8,128)(2,1)S(1)} all-gather(bf16[1,128,768]{2,1,0:T(8,128)(2,1)} %get-tuple-element.333), channel_id=4, replica_groups=mesh['dp'=8,'tensor'=4] {'tensor'}, dimensions={1}, use_global_device_ids=true | all-gather | bytes 983040 | tf_op jit(solution)/shard_map/all_gather | solution.py:127
  161.3 11.8 %all-gather.3 = s32[4,1,128]{2,1,0:T(1,128)S(1)} all-gather(s32[1,1,128]{2,1,0:T(1,128)S(1)} %copy-done.152), channel_id=5, replica_groups=mesh['dp'=8,'tensor'=4] {'tensor'}, dimensions={0}, use_global_device_ids=true | all-gather | bytes 2560 | tf_op jit(solution)/shard_map/all_gather | solution.py:128
  176.9 19.5 %all-gather.4 = bf16[1,512,768]{2,1,0:T(8,128)(2,1)S(1)} all-gather(bf16[1,128,768]{2,1,0:T(8,128)(2,1)} %get-tuple-element.332), channel_id=6, replica_groups=mesh['dp'=8,'tensor'=4] {'tensor'}, dimensions={1}, use_global_device_ids=true | all-gather | bytes 983040 | tf_op jit(solution)/shard_map/all_gather | solution.py:127
  200.7 9.3 %all-gather.5 = s32[4,1,128]{2,1,0:T(1,128)S(1)} all-gather(s32[1,1,128]{2,1,0:T(1,128)S(1)} %copy-done.151), channel_id=7, replica_groups=mesh['dp'=8,'tensor'=4] {'tensor'}, dimensions={0}, use_global_device_ids=true | all-gather | bytes 2560 | tf_op jit(solution)/shard_map/all_gather | solution.py:128
  216.9 41.4 %all-reduce.16 = (bf16[768]{0:T(1024)(128)(2,1)S(1)}, bf16[768]{0:T(1024)(128)(2,1)S(1)}, bf16[768]{0:T(1024)(128)(2,1)S(1)}, bf16[3072]{0:T(1024)(128)(2,1)S(1)...) all-reduce(bf16[768]{0:T(1024)(128)(2,1)S(1)} %dynamic-update-slice, ...), channel_id=1, replica_groups=mesh['dp'=8,'tensor'=4] {'dp','tensor'}, use_global_device_ids=true, to_apply=%add | all-reduce | flops 7680 | bytes 30720
  264.3 18.8 %all_gather.100 = bf16[512,768]{1,0:T(8,128)(2,1)} all-gather(bf16[128,768]{1,0:T(8,128)(2,1)S(1)} %get-tuple-element.338), channel_id=1, replica_groups=mesh['dp'=8,'tensor'=4] {'tensor'}, dimensions={0}, use_global_device_ids=true | all-gather | bytes 983040 | tf_op jit(solution)/shard_map/all_gather | solution.py:171
  283.1 7.2 multiply_convert_fusion.2
  293.9 24.5 %all_gather.109 = bf16[512,768]{1,0:T(8,128)(2,1)S(1)} all-gather(bf16[128,768]{1,0:T(8,128)(2,1)} %get-tuple-element.339), channel_id=1, replica_groups=mesh['dp'=8,'tensor'=4] {'tensor'}, dimensions={0}, use_global_device_ids=true | all-gather | bytes 983040 | tf_op jit(solution)/shard_map/all_gather | solution.py:171
  318.4 6.8 multiply_convert_fusion.1
  328.1 21.7 %all_gather.112 = bf16[512,768]{1,0:T(8,128)(2,1)S(1)} all-gather(bf16[128,768]{1,0:T(8,128)(2,1)} %get-tuple-element.340), channel_id=1, replica_groups=mesh['dp'=8,'tensor'=4] {'tensor'}, dimensions={0}, use_global_device_ids=true | all-gather | bytes 983040 | tf_op jit(solution)/shard_map/all_gather | solution.py:171
  349.8 6.7 multiply_convert_fusion
  367.1 12.1 %reduce-scatter.28.cloned.1.call-done = f32[128,768]{1,0:T(8,128)} async-done(((f32[512,768]{1,0:T(8,128)}), f32[128,768]{1,0:T(8,128)}) %reduce-scatter.28.cloned.1.call-update) | async-done | bytes 393232 | tf_op jit(solution)/shard_map/reduce_scatter | solution.py:174
  379.2 36.4 %reduce-scatter.32.cloned.1.call-done = f32[128,768]{1,0:T(8,128)} async-done(((f32[512,768]{1,0:T(8,128)}), f32[128,768]{1,0:T(8,128)}) %reduce-scatter.32.cloned.1.call-update) | async-done | bytes 393232 | tf_op jit(solution)/shard_map/reduce_scatter | solution.py:174
  422.4 18.2 %all_gather.113 = bf16[512,768]{1,0:T(8,128)(2,1)S(1)} all-gather(bf16[128,768]{1,0:T(8,128)(2,1)S(1)} %get-tuple-element.293), channel_id=1, replica_groups=mesh['dp'=8,'tensor'=4] {'tensor'}, dimensions={0}, use_global_device_ids=true | all-gather | bytes 983040 | tf_op jit(solution)/shard_map/all_gather | solution.py:203
  450.6 28.3 %all_gather.115 = bf16[512,768]{1,0:T(8,128)(2,1)S(1)} all-gather(bf16[128,768]{1,0:T(8,128)(2,1)S(1)} %get-tuple-element.363), channel_id=1, replica_groups=mesh['dp'=8,'tensor'=4] {'tensor'}, dimensions={0}, use_global_device_ids=true | all-gather | bytes 983040 | tf_op jit(solution)/shard_map/all_gather | solution.py:203
  485.5 20.2 %all_gather.114 = bf16[512,768]{1,0:T(8,128)(2,1)S(1)} all-gather(bf16[128,768]{1,0:T(8,128)(2,1)} %get-tuple-element.297), channel_id=1, replica_groups=mesh['dp'=8,'tensor'=4] {'tensor'}, dimensions={0}, use_global_device_ids=true | all-gather | bytes 983040 | tf_op jit(solution)/shard_map/all_gather | solution.py:203
  505.7 4.3 convert_reduce_fusion.1
  518.5 12.6 %reduce-scatter.42.cloned.1.call-done = f32[128,768]{1,0:T(8,128)} async-done(((f32[512,768]{1,0:T(8,128)}), f32[128,768]{1,0:T(8,128)}) %reduce-scatter.42.cloned.1.call-update) | async-done | bytes 393232 | tf_op jit(solution)/shard_map/reduce_scatter | solution.py:218
  535.9 32.5 %reduce-scatter.38.cloned.1.call-done = f32[128,768]{1,0:T(8,128)} async-done(((f32[512,768]{1,0:T(8,128)}), f32[128,768]{1,0:T(8,128)}) %reduce-scatter.38.cloned.1.call-update) | async-done | bytes 393232 | tf_op jit(solution)/shard_map/reduce_scatter | solution.py:218
  586.6 5.1 collective-permute-done.3
  594.2 6.0 collective-permute-done
  667.4 4.2 copy.281
  671.7 4.7 reshape.805
  693.8 39.5 %all-reduce.15 = (f32[2,768]{1,0:T(2,128)S(1)}, f32[768]{0:T(1024)S(1)}, f32[768]{0:T(1024)S(1)}, f32[768]{0:T(1024)S(1)}, f32[3072]{0:T(1024)S(1)}, /*index=5*/...) all-reduce(f32[2,768]{1,0:T(2,128)S(1)} %dynamic_update_slice.86, ...), channel_id=21, replica_groups=mesh['dp'=8,'tensor'=4] {'dp','tensor'}, use_global_device_ids=true, to_apply=%region_55.56.clone | all-reduce | flops 9216 | bytes 73728
  744.8 40.9 %reduce-scatter.50.cloned.1.call-done = f32[96,576]{1,0:T(8,128)} async-done(((f32[768,576]{1,0:T(8,128)}), f32[96,576]{1,0:T(8,128)}) %reduce-scatter.50.cloned.1.call-update) | async-done | bytes 221200
  787.6 44.6 %reduce-scatter.46.cloned.1.call-done = f32[96,768]{1,0:T(8,128)} async-done(((f32[768,768]{1,0:T(8,128)}), f32[96,768]{1,0:T(8,128)}) %reduce-scatter.46.cloned.1.call-update) | async-done | bytes 294928 | tf_op jit(solution)/shard_map/reduce_scatter | solution.py:327
  832.2 46.1 %reduce-scatter.48.cloned.1.call-done = f32[768,96]{0,1:T(8,128)} async-done(((f32[768,768]{0,1:T(8,128)}), f32[768,96]{0,1:T(8,128)}) %reduce-scatter.48.cloned.1.call-update) | async-done | bytes 294928 | tf_op jit(solution)/shard_map/reduce_scatter | solution.py:328
  (652 shorter events, 204.9 us)
Async XLA Ops:
  8.0 252.1 %reduce-scatter.22.cloned.1.call-start = ((), (), s32[]{:S(2)}) async-start(), calls=%async_computation.16 | async-start | bytes 1966080 | tf_op jit(solution)/shard_map/reduce_scatter | solution.py:163
  44.6 113.1 %copy-start.63 = (bf16[3,768,192]{2,0,1:T(4,128)(2,1)}, bf16[3,768,192]{2,0,1:T(4,128)(2,1)S(1)}, u32[]{:S(2)}) copy-start(bf16[3,768,192]{2,0,1:T(4,128)(2,1)S(1)} %all_gather.92) | copy-start | bytes 2654212
  54.9 76.5 %copy-start.54 = (bf16[4,128,3,64]{1,0,3,2:T(4,128)(2,1)}, bf16[4,128,3,64]{1,0,3,2:T(4,128)(2,1)S(1)}, u32[]{:S(2)}) copy-start(bf16[4,128,3,64]{1,0,3,2:T(4,128)(2,1)S(1)} %convert_element_type.351) | copy-start | bytes 589828
  55.1 76.5 %copy-start.15 = (f32[4,128,3,64]{1,0,3,2:T(4,128)}, f32[4,128,3,64]{1,0,3,2:T(4,128)S(1)}, u32[]{:S(2)}) copy-start(f32[4,128,3,64]{1,0,3,2:T(4,128)S(1)} %squeeze.122) | copy-start | bytes 1179652
  134.4 125.8 %reduce-scatter.26.cloned.1.call-start = ((), (), s32[]{:S(2)}) async-start(), calls=%async_computation.20 | async-start | bytes 1966080 | tf_op jit(solution)/shard_map/reduce_scatter | solution.py:163
  176.9 83.3 %reduce-scatter.30.cloned.1.call-start = ((), (), s32[]{:S(2)}) async-start(), calls=%async_computation.22 | async-start | bytes 1966080 | tf_op jit(solution)/shard_map/reduce_scatter | solution.py:163
  213.8 69.3 %all-gather.10.cloned.1.call-start = ((), (), s32[]{:S(2)}) async-start(), calls=%async_computation.17 | async-start | bytes 1327104 | tf_op jit(solution)/shard_map/all_gather | solution.py:101
  214.4 75.9 %all-gather.12.cloned.1.call-start = ((), (), s32[]{:S(2)}) async-start(), calls=%async_computation.18 | async-start | bytes 1327104 | tf_op jit(solution)/shard_map/all_gather | solution.py:102
  215.0 152.1 %reduce-scatter.24.cloned.1.call-start = ((), (), s32[]{:S(2)}) async-start(), calls=%async_computation.19 | async-start | bytes 1966080 | tf_op jit(solution)/shard_map/reduce_scatter | solution.py:174
  293.9 85.3 %reduce-scatter.28.cloned.1.call-start = ((), (), s32[]{:S(2)}) async-start(), calls=%async_computation.21 | async-start | bytes 1966080 | tf_op jit(solution)/shard_map/reduce_scatter | solution.py:174
  328.0 87.6 %reduce-scatter.32.cloned.1.call-start = ((), (), s32[]{:S(2)}) async-start(), calls=%async_computation.23 | async-start | bytes 1966080 | tf_op jit(solution)/shard_map/reduce_scatter | solution.py:174
  359.4 157.4 %reduce-scatter.34.cloned.1.call-start = ((), (), s32[]{:S(2)}) async-start(), calls=%async_computation.24 | async-start | bytes 1966080 | tf_op jit(solution)/shard_map/reduce_scatter | solution.py:218
  445.3 85.8 %reduce-scatter.42.cloned.1.call-start = ((), (), s32[]{:S(2)}) async-start(), calls=%async_computation.28 | async-start | bytes 1966080 | tf_op jit(solution)/shard_map/reduce_scatter | solution.py:218
  485.4 82.9 %reduce-scatter.38.cloned.1.call-start = ((), (), s32[]{:S(2)}) async-start(), calls=%async_computation.26 | async-start | bytes 1966080 | tf_op jit(solution)/shard_map/reduce_scatter | solution.py:218
  512.9 225.2 %reduce-scatter.52.cloned.1.call-start = ((), (), s32[]{:S(2)}) async-start(), calls=%async_computation.33 | async-start | bytes 884736
  573.4 9.7 %collective-permute-start.6 = (bf16[128,768]{1,0:T(8,128)(2,1)S(1)}, bf16[128,768]{1,0:T(8,128)(2,1)S(1)}, u32[]{:S(2)}, u32[]{:S(2)}) collective-permute-start(bf16[128,768]{1,0:T(8,128)(2,1)S(1)} %get-tuple-element.300), channel_id=1, source_target_pairs={{0,1},{1,2},{2,3},{3,0},{4,5},{5,6},{6,7},{7,4},{8,9},{9,10},{10,1... | collective-permute-start | bytes 589832 | tf_op jit(solution)/shard_map/ppermute | solution.py:240
  573.9 28.7 %collective-permute-start.7 = (bf16[128,768]{1,0:T(8,128)(2,1)S(1)}, bf16[128,768]{1,0:T(8,128)(2,1)S(1)}, u32[]{:S(2)}, u32[]{:S(2)}) collective-permute-start(bf16[128,768]{1,0:T(8,128)(2,1)S(1)} %get-tuple-element.300), channel_id=1, source_target_pairs={{0,3},{1,0},{2,1},{3,2},{4,7},{5,4},{6,5},{7,6},{8,11},{9,8},{10,9... | collective-permute-start | bytes 589832 | tf_op jit(solution)/shard_map/ppermute | solution.py:245
  577.4 14.2 %collective-permute-start.3 = (bf16[128,768]{1,0:T(8,128)(2,1)S(1)}, bf16[128,768]{1,0:T(8,128)(2,1)}, u32[]{:S(2)}, u32[]{:S(2)}) collective-permute-start(bf16[128,768]{1,0:T(8,128)(2,1)S(1)} %get-tuple-element.296), channel_id=1, source_target_pairs={{0,1},{1,2},{2,3},{3,0},{4,5},{5,6},{6,7},{7,4},{8,9},{9,10},{10,1... | collective-permute-start | bytes 589832 | tf_op jit(solution)/shard_map/ppermute | solution.py:240
  577.5 27.9 %collective-permute-start.4 = (bf16[128,768]{1,0:T(8,128)(2,1)S(1)}, bf16[128,768]{1,0:T(8,128)(2,1)S(1)}, u32[]{:S(2)}, u32[]{:S(2)}) collective-permute-start(bf16[128,768]{1,0:T(8,128)(2,1)S(1)} %get-tuple-element.296), channel_id=1, source_target_pairs={{0,3},{1,0},{2,1},{3,2},{4,7},{5,4},{6,5},{7,6},{8,11},{9,8},{10,9... | collective-permute-start | bytes 589832 | tf_op jit(solution)/shard_map/ppermute | solution.py:245
  581.4 18.7 %collective-permute-start = (bf16[128,768]{1,0:T(8,128)(2,1)S(1)}, bf16[128,768]{1,0:T(8,128)(2,1)}, u32[]{:S(2)}, u32[]{:S(2)}) collective-permute-start(bf16[128,768]{1,0:T(8,128)(2,1)S(1)} %get-tuple-element.292), channel_id=1, source_target_pairs={{0,1},{1,2},{2,3},{3,0},{4,5},{5,6},{6,7},{7,4},{8,9},{9,10},{10,1... | collective-permute-start | bytes 589832 | tf_op jit(solution)/shard_map/ppermute | solution.py:240
  583.1 22.4 %collective-permute-start.1 = (bf16[128,768]{1,0:T(8,128)(2,1)S(1)}, bf16[128,768]{1,0:T(8,128)(2,1)S(1)}, u32[]{:S(2)}, u32[]{:S(2)}) collective-permute-start(bf16[128,768]{1,0:T(8,128)(2,1)S(1)} %get-tuple-element.292), channel_id=1, source_target_pairs={{0,3},{1,0},{2,1},{3,2},{4,7},{5,4},{6,5},{7,6},{8,11},{9,8},{10,9... | collective-permute-start | bytes 589832 | tf_op jit(solution)/shard_map/ppermute | solution.py:245
  591.7 16.8 %collective-permute-start.8 = (bf16[128,768]{1,0:T(8,128)(2,1)S(1)}, bf16[128,768]{1,0:T(8,128)(2,1)S(1)}, u32[]{:S(2)}, u32[]{:S(2)}) collective-permute-start(bf16[128,768]{1,0:T(8,128)(2,1)S(1)} %collective-permute-done.6), channel_id=1, source_target_pairs={{0,1},{1,2},{2,3},{3,0},{4,5},{5,6},{6,7},{7,4},{8,9},{9,10},{10,1... | collective-permute-start | bytes 589832 | tf_op jit(solution)/shard_map/ppermute | solution.py:240
  600.1 28.1 %collective-permute-start.5 = (bf16[128,768]{1,0:T(8,128)(2,1)}, bf16[128,768]{1,0:T(8,128)(2,1)}, u32[]{:S(2)}, u32[]{:S(2)}) collective-permute-start(bf16[128,768]{1,0:T(8,128)(2,1)} %collective-permute-done.3), channel_id=1, source_target_pairs={{0,1},{1,2},{2,3},{3,0},{4,5},{5,6},{6,7},{7,4},{8,9},{9,10},{10,1... | collective-permute-start | bytes 589832 | tf_op jit(solution)/shard_map/ppermute | solution.py:240
  602.6 27.0 %collective-permute-start.2 = (bf16[128,768]{1,0:T(8,128)(2,1)}, bf16[128,768]{1,0:T(8,128)(2,1)}, u32[]{:S(2)}, u32[]{:S(2)}) collective-permute-start(bf16[128,768]{1,0:T(8,128)(2,1)} %collective-permute-done), channel_id=1, source_target_pairs={{0,1},{1,2},{2,3},{3,0},{4,5},{5,6},{6,7},{7,4},{8,9},{9,10},{10,1... | collective-permute-start | bytes 589832 | tf_op jit(solution)/shard_map/ppermute | solution.py:240
  634.1 105.6 %reduce-scatter.44.cloned.1.call-start = ((), (), s32[]{:S(2)}) async-start(), calls=%async_computation.29 | async-start | bytes 983040 | tf_op jit(solution)/shard_map/reduce_scatter | solution.py:310
  643.4 97.3 %reduce-scatter.40.cloned.1.call-start = ((), (), s32[]{:S(2)}) async-start(), calls=%async_computation.27 | async-start | bytes 983040 | tf_op jit(solution)/shard_map/reduce_scatter | solution.py:310
  656.1 86.7 %reduce-scatter.36.cloned.1.call-start = ((), (), s32[]{:S(2)}) async-start(), calls=%async_computation.25 | async-start | bytes 983040 | tf_op jit(solution)/shard_map/reduce_scatter | solution.py:310
  662.3 123.4 %reduce-scatter.50.cloned.1.call-start = ((), (), s32[]{:S(2)}) async-start(), calls=%async_computation.32 | async-start | bytes 2211840
  676.4 155.8 %reduce-scatter.46.cloned.1.call-start = ((), (), s32[]{:S(2)}) async-start(), calls=%async_computation.30 | async-start | bytes 2654208 | tf_op jit(solution)/shard_map/reduce_scatter | solution.py:327
  682.3 196.0 %reduce-scatter.48.cloned.1.call-start = ((), (), s32[]{:S(2)}) async-start(), calls=%async_computation.31 | async-start | bytes 2654208 | tf_op jit(solution)/shard_map/reduce_scatter | solution.py:328
  689.2 51.5 %copy-start.27 = (f32[128,768]{1,0:T(8,128)S(1)}, f32[128,768]{1,0:T(8,128)}, u32[]{:S(2)}) copy-start(f32[128,768]{1,0:T(8,128)} %copy-done.26) | copy-start | bytes 1179652
  690.8 52.0 %copy-start.25 = (f32[128,768]{1,0:T(8,128)S(1)}, f32[128,768]{1,0:T(8,128)}, u32[]{:S(2)}) copy-start(f32[128,768]{1,0:T(8,128)} %copy-done.24) | copy-start | bytes 1179652
  (170 other events, 761.0 us)
Sparse Core Ops, SparseCore 0:
  134.5 43.2 reduce-scatter.21
  180.1 38.0 reduce-scatter.25
  220.5 34.6 reduce-scatter.29
  294.0 47.1 reduce-scatter.23
  343.4 35.7 reduce-scatter.27
  381.3 34.2 reduce-scatter.31
  445.5 46.5 reduce-scatter.33
  494.4 36.7 reduce-scatter.41
  533.4 34.8 reduce-scatter.37
Sparse Core Ops, SparseCore 1:
  216.2 21.4 all-gather.9
  239.4 24.0 all-gather.11
  634.2 33.1 reduce-scatter.51
  669.7 23.0 reduce-scatter.43
  695.0 23.2 reduce-scatter.39
  720.6 22.1 reduce-scatter.35
  746.0 39.6 reduce-scatter.49
  789.9 42.3 reduce-scatter.45
  836.0 42.3 reduce-scatter.47
